TPU v7x, 32 devices: a whole 2x2x4 slice. The times are simulated.
32 devices in a mesh: grp: 2 (over y), bus: 4 (over z), line: 2 (over x), scen: 2 (over core).
Axes of the slice: x: 2, y: 2, z: 4, core: 2. Of those that a mesh axis runs over, the one named last changes fastest.
Arguments:
- injections: float32 [128, 4, 4096], P(('grp', 'bus', 'scen'), None, 'line'), parts along dimension 0, may hold values from -6 to 6
- shift_factors: float32 [8192, 16384], P('line', 'bus'), may hold values from -0.046875 to 0.046875
- line_limits: int32 [8192], P('line'), may hold values from 20 to 149
- overload_cost: float32 [8192], P('line'), may hold values from 0.5 to 5
Outputs:
- line_flows: float32 [128, 8192], P(('grp', 'bus', 'scen'), 'line'), parts along dimension 0
- penalty_gradient: float32 [128, 4, 4096], P(('grp', 'bus', 'scen'), None, 'line'), parts along dimension 0
There are 2 independent parts, one for each index of `grp`. A program takes and returns all parts, laid end to end along the dimension named above; an argument that names none is the same for every part. Nothing has to cross between parts.
Inputs may be any that keep to these rules, and one draw needn't show every extreme that they name: `line_limits`: thermal limits in MW on a 100 MW base.
All inputs are finite; a program needn't handle non-finite values.
Results may differ from a plain program's by a relative error of at most 0.00011.
Values sent between devices are 32-bit elements; how exact they have to be, the bound alone decides.
No kernel may reach another device: no remote copies, remote signals or barrier semaphores. Data moves between devices by JAX's collectives and lax.ppermute only.
A program may use at most 128 MiB of HBM per device.

v0:
```python
import jax
import jax.numpy as jnp
from jax import lax
from jax.sharding import PartitionSpec as P


def contract_buses(values, factors):
    return lax.dot_general(
        values,
        factors,
        (((1,), (1,)), ((), ())),
        precision=lax.Precision.HIGHEST,
        preferred_element_type=jnp.float32,
    )


def penalty_slopes(flows_part, line_limits, overload_cost):
    limits = line_limits.astype(jnp.float32) / 100.0
    excess = jax.nn.relu(flows_part - limits) - jax.nn.relu(-flows_part - limits)
    return 2.0 * overload_cost * excess


def on_device(injections, shift_factors, line_limits, overload_cost):
    widened = lax.all_gather(injections, "line", axis=2, tiled=True)
    relayed = lax.all_to_all(widened, "bus", split_axis=1, concat_axis=0, tiled=True)
    partial_flows = contract_buses(relayed[:, 0, :], shift_factors)
    group_rows = partial_flows.shape[0]
    own_count = group_rows // lax.axis_size("bus")
    summed = lax.psum(partial_flows, "bus")
    group_slopes = penalty_slopes(summed, line_limits, overload_cost)
    line_flows = lax.dynamic_slice_in_dim(summed, lax.axis_index("bus") * own_count, own_count, 0)
    partial_grad = jnp.dot(
        group_slopes,
        shift_factors,
        precision=lax.Precision.HIGHEST,
        preferred_element_type=jnp.float32,
    )
    reduced = lax.psum_scatter(partial_grad, "line", scatter_dimension=1, tiled=True)
    penalty_gradient = lax.all_to_all(
        reduced[:, None, :], "bus", split_axis=0, concat_axis=1, tiled=True
    )
    return (line_flows, penalty_gradient)


def solution(mesh):
    in_specs = (P(("grp", "bus", "scen"), None, "line"), P("line", "bus"), P("line"), P("line"))
    out_specs = (P(("grp", "bus", "scen"), "line"), P(("grp", "bus", "scen"), None, "line"))
    return jax.shard_map(
        on_device, mesh=mesh, in_specs=in_specs, out_specs=out_specs, check_vma=False
    )
```

profile of v0, /device:TPU:0, one launch (start us, length us, event | category | flops | bytes accessed | tf_op | source)
XLA Modules:
  0.0 223.7 jit_solution(5629796355818969370)
XLA Ops:
  7.2 0.0 copy-start.1
  7.2 0.0 copy-start
  7.2 0.0 all-reduce.2.cloned.1.call-start
  7.2 1.1 copy.9
  8.3 9.9 %all_gather.3 = f32[8,4,4096]{2,0,1:T(8,128)S(1)} all-gather(f32[8,4,2048]{2,0,1:T(8,128)S(1)} %copy.9), channel_id=1, replica_groups=mesh['grp'=2,'bus'=4,'line'=2,'scen'=2] {'line'}, dimensions={2}, use_global_device_ids=true | all-gather | bytes 786432 | tf_op jit(solution)/shard_map/all_gather | solution.py:24
  18.3 18.5 %all_to_all.33 = f32[8,4,4096]{2,0,1:T(8,128)S(1)} all-to-all(f32[8,4,4096]{2,0,1:T(8,128)S(1)} %all_gather.3), channel_id=1, replica_groups=mesh['grp'=2,'bus'=4,'line'=2,'scen'=2] {'bus'}, dimensions={1} | all-to-all | bytes 1048576 | tf_op jit(solution)/shard_map/all_to_all | solution.py:25
  36.8 66.5 %fusion = f32[32,4096]{1,0:T(8,128)} fusion(f32[4096,4096]{1,0:T(8,128)} %param.5, f32[8,4,4096]{2,0,1:T(8,128)S(1)} %all_to_all.33), kind=kOutput, calls=%fused_computation | convolution fusion | flops 6442450944 | bytes 68157440 | tf_op jit(solution)/shard_map/dot_general | solution.py:8
  103.3 0.0 all-reduce.2.cloned.1.call-update
  103.4 0.2 reduce-scatter.2.cloned.1.call-start
  103.6 0.0 copy-done.1
  103.6 0.0 copy-done
  103.6 37.6 %all-reduce.2.cloned.1.call-done = f32[32,4096]{1,0:T(8,128)} async-done(((f32[32,4096]{1,0:T(8,128)}), f32[32,4096]{1,0:T(8,128)}) %all-reduce.2.cloned.1.call-update) | async-done | bytes 524304 | tf_op jit(solution)/shard_map/psum | solution.py:29
  141.2 44.9 %fusion.2 = f32[32,4096]{1,0:T(8,128)} fusion(f32[4096,4096]{1,0:T(8,128)} %param.5, f32[32,4096]{1,0:T(8,128)} %all-reduce.2.cloned.1.call-done, f32[4096]{0:T(1024)S(1)} %get-tuple-element.2, f32[4096]{0:T(1024)S(1)} %get-tuple-element.3), kind=kOutput, calls=%fused_computation.2 | convolution fusion | flops 6443368448 | bytes 68190208 | tf_op jit(solution)/shard_map/dot_general | solution.py:32
  186.1 0.0 reduce-scatter.2.cloned.1.call-update
  186.2 14.6 %reduce-scatter.2.cloned.1.call-done = f32[32,2048]{1,0:T(8,128)} async-done(((f32[32,4096]{1,0:T(8,128)}), f32[32,2048]{1,0:T(8,128)}) %reduce-scatter.2.cloned.1.call-update) | async-done | bytes 262160 | tf_op jit(solution)/shard_map/reduce_scatter | solution.py:38
  200.8 1.9 copy.10
  202.7 4.6 %all-to-all-start.1 = ((f32[32,1,2048]{2,1,0:T(1,128)}), f32[32,1,2048]{2,1,0:T(1,128)S(1)}, u32[]{:S(2)}, u32[]{:S(2)}) async-start(f32[32,1,2048]{2,1,0:T(1,128)} %copy.10), calls=%async_computation.2 | async-start | bytes 524288 | tf_op jit(solution)/shard_map/all_to_all | solution.py:39
  207.3 1.6 constant_dynamic-slice_fusion
  208.9 7.2 %all-to-all-done.1 = f32[32,1,2048]{2,1,0:T(1,128)S(1)} async-done(((f32[32,1,2048]{2,1,0:T(1,128)}), f32[32,1,2048]{2,1,0:T(1,128)S(1)}, u32[]{:S(2)}, u32[]{:S(2)}) %all-to-all-start.1) | async-done | bytes 262176 | tf_op jit(solution)/shard_map/all_to_all | solution.py:39
  216.0 0.9 copy.13
  (1 shorter events, 0.0 us)
Async XLA Ops:
  7.2 96.4 %copy-start.1 = (f32[4096]{0:T(1024)S(1)}, f32[4096]{0:T(1024)}, u32[]{:S(2)}) copy-start(f32[4096]{0:T(1024)} %param.7) | copy-start | bytes 49156
  7.2 96.4 %copy-start = (s32[4096]{0:T(1024)S(1)}, s32[4096]{0:T(1024)}, u32[]{:S(2)}) copy-start(s32[4096]{0:T(1024)} %param.6) | copy-start | bytes 49156
  7.2 134.0 %all-reduce.2.cloned.1.call-start = ((), (), s32[]{:S(2)}) async-start(), calls=%async_computation.3 | async-start | bytes 1048576 | tf_op jit(solution)/shard_map/psum | solution.py:29
  103.4 97.4 %reduce-scatter.2.cloned.1.call-start = ((), (), s32[]{:S(2)}) async-start(), calls=%async_computation.4 | async-start | bytes 786432 | tf_op jit(solution)/shard_map/reduce_scatter | solution.py:38
  202.7 13.3 %all-to-all-start.1 = ((f32[32,1,2048]{2,1,0:T(1,128)}), f32[32,1,2048]{2,1,0:T(1,128)S(1)}, u32[]{:S(2)}, u32[]{:S(2)}) async-start(f32[32,1,2048]{2,1,0:T(1,128)} %copy.10), calls=%async_computation.2 | async-start | bytes 524288 | tf_op jit(solution)/shard_map/all_to_all | solution.py:39
Sparse Core Ops, SparseCore 0:
  103.5 37.6 all-reduce.1
  186.3 14.4 reduce-scatter.1
where the time goes:
time: 224 us
  matrix products  111 us (50%)
  waiting for transfers between devices  59.4 us (27%)
  blocking collectives  28.5 us (13%)
  between operations  14.1 us (6%)
  local copies, waits for them, and re-layouts  5.48 us (2%)
  starting transfers between devices  4.85 us (2%)
    dot_general x1, matrix products, contract_buses(): lax.dot_general(values, factors, (((1,), (1,)), ((), ())), precision=lax....  66.5 us
    dot_general x1, matrix products, on_device(): jnp.dot(group_slopes, shift_factors, precision=lax.Precision.HIGHEST, pre...  44.9 us
    psum x1, waiting for transfers between devices, on_device(): summed = lax.psum(partial_flows, 'bus')  37.6 us
    all_to_all x1, blocking collectives, on_device(): lax.all_to_all(widened, 'bus', split_axis=1, concat_axis=0, tiled=True)  18.5 us
    reduce_scatter x1, waiting for transfers between devices, on_device(): lax.psum_scatter(partial_grad, 'line', scatter_dimension=1, tiled=True)  14.6 us
    all_gather x1, blocking collectives, on_device(): widened = lax.all_gather(injections, 'line', axis=2, tiled=True)  9.94 us
    all_to_all x1, waiting for transfers between devices, on_device(): lax.all_to_all(reduced[:, None, :], 'bus', split_axis=0, concat_axis=1, t...  7.16 us
    all_to_all x1, starting transfers between devices, on_device(): lax.all_to_all(reduced[:, None, :], 'bus', split_axis=0, concat_axis=1, t...  4.59 us
  transfers between devices with their start and end apart: 3, of which 3 were waited for; matrix products, arithmetic and copies ran while one was open for 1% of the time, Pallas kernels for 0%

commit v1 on v0

--- a/solution.py
+++ b/solution.py
@@ -26,7 +26,8 @@
     partial_flows = contract_buses(relayed[:, 0, :], shift_factors)
     group_rows = partial_flows.shape[0]
     own_count = group_rows // lax.axis_size("bus")
-    summed = lax.psum(partial_flows, "bus")
+    shards = lax.all_gather(partial_flows, "bus")
+    summed = jnp.sum(shards, axis=0)
     group_slopes = penalty_slopes(summed, line_limits, overload_cost)
     line_flows = lax.dynamic_slice_in_dim(summed, lax.axis_index("bus") * own_count, own_count, 0)
     partial_grad = jnp.dot(

time: 224 us -> 232 us (1.036)
  waiting for transfers between devices: 59.4 us -> 66.4 us
    all_gather x0 -> x1, waiting for transfers between devices: none -> 44.7 us  [on_device(): shards = lax.all_gather(partial_flows, 'bus')]
    psum x1 -> x0, waiting for transfers between devices: 37.6 us -> none  [on_device(): summed = lax.psum(partial_flows, 'bus')]
  transfers between devices with their start and end apart: 3 -> 3, of which waited for: 3 -> 3; matrix products, arithmetic and copies ran while one was open for 1% -> 0% of each run, Pallas kernels for 0% -> 0%
where the time goes in v1:
time: 232 us
  matrix products  111 us (48%)
  waiting for transfers between devices  66.4 us (29%)
  blocking collectives  28.5 us (12%)
  between operations  14.1 us (6%)
  starting transfers between devices  4.85 us (2%)
  local copies, waits for them, and re-layouts  4.57 us (2%)
    dot_general x1, matrix products, contract_buses(): lax.dot_general(values, factors, (((1,), (1,)), ((), ())), precision=lax....  66.5 us
    dot_general x1, matrix products, on_device(): jnp.dot(group_slopes, shift_factors, precision=lax.Precision.HIGHEST, pre...  44.9 us
    all_gather x1, waiting for transfers between devices, on_device(): shards = lax.all_gather(partial_flows, 'bus')  44.7 us
    all_to_all x1, blocking collectives, on_device(): lax.all_to_all(widened, 'bus', split_axis=1, concat_axis=0, tiled=True)  18.5 us
    reduce_scatter x1, waiting for transfers between devices, on_device(): lax.psum_scatter(partial_grad, 'line', scatter_dimension=1, tiled=True)  13.6 us
    all_gather x1, blocking collectives, on_device(): widened = lax.all_gather(injections, 'line', axis=2, tiled=True)  9.94 us
    all_to_all x1, waiting for transfers between devices, on_device(): lax.all_to_all(reduced[:, None, :], 'bus', split_axis=0, concat_axis=1, t...  8.08 us
  transfers between devices with their start and end apart: 3, of which 3 were waited for; matrix products, arithmetic and copies ran while one was open for 0% of the time, Pallas kernels for 0%

profile of v1, /device:TPU:0, one launch (start us, length us, event | category | flops | bytes accessed | tf_op | source)
XLA Modules:
  0.0 231.6 jit_solution(8070750827019095575)
XLA Ops:
  7.2 0.0 copy-start
  7.2 0.0 copy-start.1
  7.2 0.0 all-gather.3.cloned.1.call-start
  7.2 1.1 copy.9
  8.3 9.9 %all_gather.9 = f32[8,4,4096]{2,0,1:T(8,128)S(1)} all-gather(f32[8,4,2048]{2,0,1:T(8,128)S(1)} %copy.9), channel_id=1, replica_groups=mesh['grp'=2,'bus'=4,'line'=2,'scen'=2] {'line'}, dimensions={2}, use_global_device_ids=true | all-gather | bytes 786432 | tf_op jit(solution)/shard_map/all_gather | solution.py:24
  18.3 18.5 %all_to_all.33 = f32[8,4,4096]{2,0,1:T(8,128)S(1)} all-to-all(f32[8,4,4096]{2,0,1:T(8,128)S(1)} %all_gather.9), channel_id=1, replica_groups=mesh['grp'=2,'bus'=4,'line'=2,'scen'=2] {'bus'}, dimensions={1} | all-to-all | bytes 1048576 | tf_op jit(solution)/shard_map/all_to_all | solution.py:25
  36.8 66.5 %fusion = f32[32,4096]{1,0:T(8,128)} fusion(f32[4096,4096]{1,0:T(8,128)} %param.5, f32[8,4,4096]{2,0,1:T(8,128)S(1)} %all_to_all.33), kind=kOutput, calls=%fused_computation | convolution fusion | flops 6442450944 | bytes 68157440 | tf_op jit(solution)/shard_map/dot_general | solution.py:8
  103.3 0.0 all-gather.3.cloned.1.call-update
  103.4 0.2 reduce-scatter.2.cloned.1.call-start
  103.6 0.0 copy-done
  103.6 0.0 copy-done.1
  103.6 44.7 %all-gather.3.cloned.1.call-done = f32[128,4096]{1,0:T(8,128)} async-done(((f32[32,4096]{1,0:T(8,128)}), f32[128,4096]{1,0:T(8,128)}) %all-gather.3.cloned.1.call-update) | async-done | bytes 2097168 | tf_op jit(solution)/shard_map/all_gather | solution.py:29
  148.3 1.8 reduce_sum.9
  150.1 44.9 %fusion.2 = f32[32,4096]{1,0:T(8,128)} fusion(f32[4096,4096]{1,0:T(8,128)} %param.5, f32[32,4096]{1,0:T(8,128)S(1)} %reduce_sum.9, f32[4096]{0:T(1024)S(1)} %get-tuple-element.2, f32[4096]{0:T(1024)S(1)} %get-tuple-element.3), kind=kOutput, calls=%fused_computation.2 | convolution fusion | flops 6443368448 | bytes 68190208 | tf_op jit(solution)/shard_map/dot_general | solution.py:33
  195.0 0.0 reduce-scatter.2.cloned.1.call-update
  195.0 13.6 %reduce-scatter.2.cloned.1.call-done = f32[32,2048]{1,0:T(8,128)} async-done(((f32[32,4096]{1,0:T(8,128)}), f32[32,2048]{1,0:T(8,128)}) %reduce-scatter.2.cloned.1.call-update) | async-done | bytes 262160 | tf_op jit(solution)/shard_map/reduce_scatter | solution.py:39
  208.6 1.9 copy.10
  210.5 4.6 %all-to-all-start.1 = ((f32[32,1,2048]{2,1,0:T(1,128)}), f32[32,1,2048]{2,1,0:T(1,128)S(1)}, u32[]{:S(2)}, u32[]{:S(2)}) async-start(f32[32,1,2048]{2,1,0:T(1,128)} %copy.10), calls=%async_computation.2 | async-start | bytes 524288 | tf_op jit(solution)/shard_map/all_to_all | solution.py:40
  215.1 0.7 constant_dynamic-slice_fusion
  215.8 8.1 %all-to-all-done.1 = f32[32,1,2048]{2,1,0:T(1,128)S(1)} async-done(((f32[32,1,2048]{2,1,0:T(1,128)}), f32[32,1,2048]{2,1,0:T(1,128)S(1)}, u32[]{:S(2)}, u32[]{:S(2)}) %all-to-all-start.1) | async-done | bytes 262176 | tf_op jit(solution)/shard_map/all_to_all | solution.py:40
  223.9 0.9 copy.13
  (1 shorter events, 0.0 us)
Async XLA Ops:
  7.2 96.4 %copy-start = (s32[4096]{0:T(1024)S(1)}, s32[4096]{0:T(1024)}, u32[]{:S(2)}) copy-start(s32[4096]{0:T(1024)} %param.6) | copy-start | bytes 49156
  7.2 96.4 %copy-start.1 = (f32[4096]{0:T(1024)S(1)}, f32[4096]{0:T(1024)}, u32[]{:S(2)}) copy-start(f32[4096]{0:T(1024)} %param.7) | copy-start | bytes 49156
  7.2 141.1 %all-gather.3.cloned.1.call-start = ((), (), s32[]{:S(2)}) async-start(), calls=%async_computation.4 | async-start | bytes 2621440 | tf_op jit(solution)/shard_map/all_gather | solution.py:29
  103.4 105.3 %reduce-scatter.2.cloned.1.call-start = ((), (), s32[]{:S(2)}) async-start(), calls=%async_computation.3 | async-start | bytes 786432 | tf_op jit(solution)/shard_map/reduce_scatter | solution.py:39
  210.5 13.3 %all-to-all-start.1 = ((f32[32,1,2048]{2,1,0:T(1,128)}), f32[32,1,2048]{2,1,0:T(1,128)S(1)}, u32[]{:S(2)}, u32[]{:S(2)}) async-start(f32[32,1,2048]{2,1,0:T(1,128)} %copy.10), calls=%async_computation.2 | async-start | bytes 524288 | tf_op jit(solution)/shard_map/all_to_all | solution.py:40
Sparse Core Ops, SparseCore 0:
  103.5 44.7 all-gather.2
  195.2 13.4 reduce-scatter.1

commit v2 on v0

--- a/solution.py
+++ b/solution.py
@@ -22,7 +22,9 @@
 
 def on_device(injections, shift_factors, line_limits, overload_cost):
     widened = lax.all_gather(injections, "line", axis=2, tiled=True)
-    relayed = lax.all_to_all(widened, "bus", split_axis=1, concat_axis=0, tiled=True)
+    pieces = jnp.split(widened, lax.axis_size("bus"), axis=1)
+    received = lax.all_to_all(jnp.stack(pieces), "bus", 0, 0)
+    relayed = jnp.concatenate(received, axis=0)
     partial_flows = contract_buses(relayed[:, 0, :], shift_factors)
     group_rows = partial_flows.shape[0]
     own_count = group_rows // lax.axis_size("bus")

time: 224 us -> 225 us (level)
  no operation moved by 1% of the time
where the time goes in v2:
time: 225 us
  matrix products  112 us (50%)
  waiting for transfers between devices  59.3 us (26%)
  blocking collectives  28.7 us (13%)
  between operations  14.1 us (6%)
  starting transfers between devices  4.85 us (2%)
  local copies, waits for them, and re-layouts  4.81 us (2%)
    dot_general x1, matrix products, contract_buses(): lax.dot_general(values, factors, (((1,), (1,)), ((), ())), precision=lax....  67.3 us
    dot_general x1, matrix products, on_device(): jnp.dot(group_slopes, shift_factors, precision=lax.Precision.HIGHEST, pre...  44.9 us
    psum x1, waiting for transfers between devices, on_device(): summed = lax.psum(partial_flows, 'bus')  37.5 us
    all_to_all x1, blocking collectives, on_device(): received = lax.all_to_all(jnp.stack(pieces), 'bus', 0, 0)  18.5 us
    reduce_scatter x1, waiting for transfers between devices, on_device(): lax.psum_scatter(partial_grad, 'line', scatter_dimension=1, tiled=True)  14.6 us
    all_gather x1, blocking collectives, on_device(): widened = lax.all_gather(injections, 'line', axis=2, tiled=True)  10.2 us
    all_to_all x1, waiting for transfers between devices, on_device(): lax.all_to_all(reduced[:, None, :], 'bus', split_axis=0, concat_axis=1, t...  7.16 us
    all_to_all x1, starting transfers between devices, on_device(): lax.all_to_all(reduced[:, None, :], 'bus', split_axis=0, concat_axis=1, t...  4.59 us
  transfers between devices with their start and end apart: 3, of which 3 were waited for; matrix products, arithmetic and copies ran while one was open for 1% of the time, Pallas kernels for 0%

profile of v2, /device:TPU:0, one launch (start us, length us, event | category | flops | bytes accessed | tf_op | source)
XLA Modules:
  0.0 224.6 jit_solution(3707033856214736309)
XLA Ops:
  7.2 0.0 copy-start.1
  7.2 0.0 copy-start
  7.2 0.0 all-reduce.2.cloned.1.call-start
  7.2 10.2 %all_gather.3 = f32[8,4,4096]{2,1,0:T(4,128)S(1)} all-gather(f32[8,4,2048]{2,1,0:T(4,128)} %param.4), channel_id=1, replica_groups=mesh['grp'=2,'bus'=4,'line'=2,'scen'=2] {'line'}, dimensions={2}, use_global_device_ids=true | all-gather | bytes 786432 | tf_op jit(solution)/shard_map/all_gather | solution.py:24
  17.4 0.4 slice_bitcast_fusion.3
  17.9 0.5 pad_maximum_fusion
  18.4 18.5 %all_to_all.23 = f32[4,8,1,4096]{3,2,1,0:T(1,128)S(1)} all-to-all(f32[4,8,1,4096]{3,2,1,0:T(1,128)S(1)} %pad_maximum_fusion), channel_id=1, replica_groups=mesh['grp'=2,'bus'=4,'line'=2,'scen'=2] {'bus'}, dimensions={0} | all-to-all | bytes 1048576 | tf_op jit(solution)/shard_map/all_to_all | solution.py:26
  36.9 67.3 %fusion = f32[32,4096]{1,0:T(8,128)} fusion(f32[4096,4096]{1,0:T(8,128)} %param.5, f32[4,8,1,4096]{3,2,1,0:T(1,128)S(1)} %all_to_all.23), kind=kOutput, calls=%fused_computation.1 | convolution fusion | flops 6442450944 | bytes 68157440 | tf_op jit(solution)/shard_map/dot_general | solution.py:8
  104.2 0.0 all-reduce.2.cloned.1.call-update
  104.3 0.2 reduce-scatter.2.cloned.1.call-start
  104.5 0.0 copy-done.1
  104.5 0.0 copy-done
  104.5 37.5 %all-reduce.2.cloned.1.call-done = f32[32,4096]{1,0:T(8,128)} async-done(((f32[32,4096]{1,0:T(8,128)}), f32[32,4096]{1,0:T(8,128)}) %all-reduce.2.cloned.1.call-update) | async-done | bytes 524304 | tf_op jit(solution)/shard_map/psum | solution.py:31
  142.1 44.9 %fusion.3 = f32[32,4096]{1,0:T(8,128)} fusion(f32[4096,4096]{1,0:T(8,128)} %param.5, f32[32,4096]{1,0:T(8,128)} %all-reduce.2.cloned.1.call-done, f32[4096]{0:T(1024)S(1)} %get-tuple-element.6, f32[4096]{0:T(1024)S(1)} %get-tuple-element.7), kind=kOutput, calls=%fused_computation.4 | convolution fusion | flops 6443368448 | bytes 68190208 | tf_op jit(solution)/shard_map/dot_general | solution.py:34
  187.0 0.0 reduce-scatter.2.cloned.1.call-update
  187.0 14.6 %reduce-scatter.2.cloned.1.call-done = f32[32,2048]{1,0:T(8,128)} async-done(((f32[32,4096]{1,0:T(8,128)}), f32[32,2048]{1,0:T(8,128)}) %reduce-scatter.2.cloned.1.call-update) | async-done | bytes 262160 | tf_op jit(solution)/shard_map/reduce_scatter | solution.py:40
  201.6 1.9 copy.7
  203.6 4.6 %all-to-all-start.1 = ((f32[32,1,2048]{2,1,0:T(1,128)}), f32[32,1,2048]{2,1,0:T(1,128)S(1)}, u32[]{:S(2)}, u32[]{:S(2)}) async-start(f32[32,1,2048]{2,1,0:T(1,128)} %copy.7), calls=%async_computation.2 | async-start | bytes 524288 | tf_op jit(solution)/shard_map/all_to_all | solution.py:41
  208.2 1.6 constant_dynamic-slice_fusion
  209.7 7.2 %all-to-all-done.1 = f32[32,1,2048]{2,1,0:T(1,128)S(1)} async-done(((f32[32,1,2048]{2,1,0:T(1,128)}), f32[32,1,2048]{2,1,0:T(1,128)S(1)}, u32[]{:S(2)}, u32[]{:S(2)}) %all-to-all-start.1) | async-done | bytes 262176 | tf_op jit(solution)/shard_map/all_to_all | solution.py:41
  216.9 0.9 copy.15
  (1 shorter events, 0.0 us)
Async XLA Ops:
  7.2 97.3 %copy-start.1 = (f32[4096]{0:T(1024)S(1)}, f32[4096]{0:T(1024)}, u32[]{:S(2)}) copy-start(f32[4096]{0:T(1024)} %param.7) | copy-start | bytes 49156
  7.2 97.3 %copy-start = (s32[4096]{0:T(1024)S(1)}, s32[4096]{0:T(1024)}, u32[]{:S(2)}) copy-start(s32[4096]{0:T(1024)} %param.6) | copy-start | bytes 49156
  7.2 134.9 %all-reduce.2.cloned.1.call-start = ((), (), s32[]{:S(2)}) async-start(), calls=%async_computation.3 | async-start | bytes 1048576 | tf_op jit(solution)/shard_map/psum | solution.py:31
  104.3 97.4 %reduce-scatter.2.cloned.1.call-start = ((), (), s32[]{:S(2)}) async-start(), calls=%async_computation.4 | async-start | bytes 786432 | tf_op jit(solution)/shard_map/reduce_scatter | solution.py:40
  203.6 13.3 %all-to-all-start.1 = ((f32[32,1,2048]{2,1,0:T(1,128)}), f32[32,1,2048]{2,1,0:T(1,128)S(1)}, u32[]{:S(2)}, u32[]{:S(2)}) async-start(f32[32,1,2048]{2,1,0:T(1,128)} %copy.7), calls=%async_computation.2 | async-start | bytes 524288 | tf_op jit(solution)/shard_map/all_to_all | solution.py:41
Sparse Core Ops, SparseCore 0:
  104.4 37.6 all-reduce.1
  187.2 14.4 reduce-scatter.1
